TPU v7x, 128 devices: a whole 4x4x4 slice. The times are simulated.
128 devices in a mesh: leaf: 32 (over z, y, core), rows: 4 (over x).
Axes of the slice: x: 4, y: 4, z: 4, core: 2. Of those that a mesh axis runs over, the one named last changes fastest.
Arguments:
- child_update: float32 [32, 512, 512], P('leaf', 'rows'), as said below
- block_maps: int32 [3, 32, 4], replicated, may hold values from 0 to 11, as said below
- sep_share: float32 [32, 3, 1024, 1024], P('leaf', None, 'rows'), as said below
- coupling_share: float32 [32, 3, 512, 1024], P('leaf', None, 'rows')
Outputs:
- diag_factor: float32 [32, 3, 1024, 1024], P('leaf', None, 'rows')
- below_factor: float32 [32, 3, 512, 1024], P('leaf', None, 'rows')
- top_update: float32 [32, 512, 512], P('leaf', 'rows')
Inputs may be any that keep to these rules, and one draw needn't show every extreme that they name: Each row block_maps[k, c] names 4 different front blocks; at every level k, the rows 2g and 2g+1 together name every block from 8 on. At level k only the rows c < 32 / 2^k are used. `child_update`: Symmetric. `sep_share`: symmetric in its last two dimensions.
All inputs are finite; a program needn't handle non-finite values.
Results may differ from a plain program's by a relative error of at most 0.00012.
Values sent between devices are 32-bit elements; how exact they have to be, the bound alone decides.
No kernel may reach another device: no remote copies, remote signals or barrier semaphores. Data moves between devices by JAX's collectives and lax.ppermute only.
A program may use at most 192 MiB of HBM per device.

v0:
```python
import jax
import jax.numpy as jnp
from jax import lax
from jax.sharding import PartitionSpec as P

BLK = 128
LEVELS = 3


highest = lax.Precision.HIGHEST


def partner(x, axis, stride):
    return lax.ppermute(x, axis, [(i, i ^ 1 << stride) for i in range(lax.axis_size(axis))])


def block_cholesky(matrix):
    order = matrix.shape[-1]
    if order <= 512:
        return jnp.linalg.cholesky(matrix, symmetrize_input=False)
    half = order // 2
    top_factor = block_cholesky(matrix[:half, :half])
    lower_panel = lax.linalg.triangular_solve(
        top_factor, matrix[half:, :half], left_side=False, lower=True, transpose_a=True
    )
    remainder = matrix[half:, half:] - jnp.dot(
        lower_panel, lower_panel.T, precision=highest, preferred_element_type=jnp.float32
    )
    bottom_factor = block_cholesky(remainder)
    upper_zero = jnp.zeros((half, order - half), jnp.float32)
    top_rows = jnp.concatenate([top_factor, upper_zero], axis=1)
    bottom_rows = jnp.concatenate([lower_panel, bottom_factor], axis=1)
    return jnp.concatenate([top_rows, bottom_rows], axis=0)


def sym_cholesky(matrix):
    return block_cholesky((matrix + matrix.T) * 0.5)


def place_columns(portion, block_map, blocks_front):
    count_rows = portion.shape[0]
    blocks_child = block_map.shape[0]
    selector = (block_map[None, :] == jnp.arange(blocks_front, dtype=jnp.int32)[:, None]).astype(
        jnp.float32
    )
    placed = jnp.einsum(
        "qm,nmb->nqb", selector, portion.reshape(count_rows, blocks_child, BLK), precision=highest
    )
    return placed.reshape(count_rows, blocks_front * BLK)


def pick_rows(portion, block_map, global_rows):
    count_rows = portion.shape[0]
    blocks_child = block_map.shape[0]
    matches = (block_map[None, :] == (global_rows // BLK)[:, None]).astype(jnp.int32)
    found = jnp.sum(matches, axis=1) > 0
    source_block = jnp.sum(matches * jnp.arange(blocks_child, dtype=jnp.int32)[None, :], axis=1)
    source_row = source_block * BLK + global_rows % BLK
    usable = found & (source_row >= 0) & (source_row < count_rows)
    picked = jnp.take(portion, jnp.clip(source_row, 0, count_rows - 1), axis=0)
    return jnp.where(usable[:, None], picked, 0.0)


def on_device(child_update, block_maps, sep_share, coupling_share):
    upd_rows = child_update.shape[1]
    upd_width = child_update.shape[2]
    sep_rows = sep_share.shape[2]
    sep_width = sep_share.shape[3]
    front_width = sep_width + upd_width
    blocks_front = front_width // BLK
    leaf_index = lax.axis_index("leaf")
    row_id = lax.axis_index("rows")
    targets = jnp.concatenate(
        [
            row_id * sep_rows + jnp.arange(sep_rows, dtype=jnp.int32),
            sep_width + row_id * upd_rows + jnp.arange(upd_rows, dtype=jnp.int32),
        ]
    )
    current = child_update[0]
    pend_sep = sep_share[0]
    pend_cpl = coupling_share[0]
    diag_parts = []
    below_parts = []
    for level_index in range(LEVELS):
        partner_rows, got_sep, got_cpl = partner((current, pend_sep, pend_cpl), "leaf", level_index)
        pend_sep = pend_sep + got_sep
        pend_cpl = pend_cpl + got_cpl
        sep_orig = pend_sep[0]
        cpl_orig = pend_cpl[0]
        pend_sep = pend_sep[1:]
        pend_cpl = pend_cpl[1:]
        is_right = leaf_index >> level_index & 1
        left_rows = jnp.where(is_right == 0, current, partner_rows)
        right_rows = jnp.where(is_right == 0, partner_rows, current)
        first_child = (leaf_index >> level_index + 1) * 2
        left_map = lax.dynamic_index_in_dim(block_maps[level_index], first_child, 0, keepdims=False)
        right_map = lax.dynamic_index_in_dim(
            block_maps[level_index], first_child + 1, 0, keepdims=False
        )

        def add_children(running, portions, offset, left_map=left_map, right_map=right_map):
            for portion, block_map in ((portions[0], left_map), (portions[1], right_map)):
                running = running + place_columns(
                    pick_rows(portion, block_map, targets), block_map, blocks_front
                )
            return running

        front_rows = add_children(
            jnp.zeros((sep_rows + upd_rows, front_width), jnp.float32),
            (
                lax.all_gather(left_rows, "rows", axis=0, tiled=True),
                lax.all_gather(right_rows, "rows", axis=0, tiled=True),
            ),
            jnp.int32(0),
        )
        front_pivot = front_rows[:sep_rows, :sep_width] + sep_orig
        front_below = front_rows[sep_rows:, :sep_width] + cpl_orig
        front_trail = front_rows[sep_rows:, sep_width:]
        pivot_block = lax.all_gather(front_pivot, "rows", axis=0, tiled=True)
        pivot_factor = sym_cholesky(pivot_block)
        solved = lax.linalg.triangular_solve(
            pivot_factor, front_below, left_side=False, lower=True, transpose_a=True
        )
        left_part = solved

        def product(portion, offset, left_part=left_part):
            return -jnp.dot(
                left_part, portion.T, precision=highest, preferred_element_type=jnp.float32
            )

        schur_part = front_trail + product(
            lax.all_gather(solved, "rows", axis=0, tiled=True), jnp.int32(0)
        )
        diag_parts.append(lax.dynamic_slice_in_dim(pivot_factor, row_id * sep_rows, sep_rows, 0))
        below_parts.append(solved)
        current = schur_part
    return (jnp.stack(diag_parts)[None], jnp.stack(below_parts)[None], current[None])


def solution(mesh):
    return jax.shard_map(
        on_device,
        mesh=mesh,
        in_specs=(
            P("leaf", "rows", None),
            P(),
            P("leaf", None, "rows", None),
            P("leaf", None, "rows", None),
        ),
        out_specs=(
            P("leaf", None, "rows", None),
            P("leaf", None, "rows", None),
            P("leaf", "rows", None),
        ),
        check_vma=False,
    )
```

profile of v0, /device:TPU:1, one launch (start us, length us, event | category | flops | bytes accessed | tf_op | source)
XLA Modules:
  0.0 1728.2 jit_solution(13907045781276301136)
XLA Ops:
  17.3 19.9 %all-gather.15.cloned.1.call-done = f32[512,512]{1,0:T(8,128)} async-done(((f32[128,512]{1,0:T(8,128)}), f32[512,512]{1,0:T(8,128)}) %all-gather.15.cloned.1.call-update) | async-done | bytes 1048592 | tf_op jit(solution)/shard_map/all_gather | solution.py:112
  41.9 21.4 %all-gather.13.cloned.1.call-done = f32[512,512]{1,0:T(8,128)} async-done(((f32[128,512]{1,0:T(8,128)}), f32[512,512]{1,0:T(8,128)}) %all-gather.13.cloned.1.call-update) | async-done | bytes 1048592 | tf_op jit(solution)/shard_map/all_gather | solution.py:111
  92.3 36.4 %all-gather.17.cloned.1.call-done = f32[1024,1024]{0,1:T(8,128)} async-done(((f32[256,1024]{0,1:T(8,128)}), f32[1024,1024]{0,1:T(8,128)}) %all-gather.17.cloned.1.call-update) | async-done | bytes 4194320 | tf_op jit(solution)/shard_map/all_gather | solution.py:119
  252.3 40.1 %custom-call.48 = f32[4,128,128]{1,2,0:T(8,128)S(1)} custom-call(f32[4,128,128]{2,1,0:T(8,128)} %copy-done.32), custom_call_target="InvertDiagBlocksLowerTriangular" | custom-call | tf_op jit(solution)/shard_map/triangular_solve/custom-call.3 | solution.py:23
  372.8 13.2 cholesky.759
  427.3 28.5 %while.13 = (s32[]{:T(128)}, f32[1024,1024]{1,0:T(8,128)}, s32[8,2]{0,1:T(2,128)S(1)}, f32[8,128,128]{2,1,0:T(8,128)}, s32[]{:T(128)}) while((s32[]{:T(128)}, f32[1024,1024]{1,0:T(8,128)}, s32[8,2]{0,1:T(2,128)S(1)}, f32[8,128,128]{2,1,0:T(8,128)}, s32[]{:T(128)}) %tuple.250), condition=%wide.while_cond.1, body=%wide.while_body.1.sunk | while | flops 2 | bytes 132205 | solution.py:121
  455.8 80.2 %custom-call.52 = f32[8,128,128]{1,2,0:T(8,128)} custom-call(f32[8,128,128]{2,1,0:T(8,128)} %get-tuple-element.48), custom_call_target="InvertDiagBlocksLowerTriangular" | custom-call | tf_op jit(solution)/shard_map/triangular_solve/custom-call.8 | solution.py:121
  559.8 34.0 %all-gather.19.cloned.1.call-done = f32[512,1024]{0,1:T(8,128)} async-done(((f32[128,1024]{0,1:T(8,128)}), f32[512,1024]{0,1:T(8,128)}) %all-gather.19.cloned.1.call-update) | async-done | bytes 2097168 | tf_op jit(solution)/shard_map/all_gather | solution.py:132
  610.1 43.6 %collective-permute-done.4 = f32[2,256,1024]{1,2,0:T(8,128)} collective-permute-done((f32[2,256,1024]{1,2,0:T(8,128)}, f32[2,256,1024]{1,2,0:T(8,128)}, u32[]{:S(2)}, u32[]{:S(2)}) %collective-permute-start.4) | collective-permute-done | bytes 2097184 | tf_op jit(solution)/shard_map/ppermute | solution.py:14
  681.5 22.2 %collective-permute-done.5 = f32[2,128,1024]{1,2,0:T(8,128)S(1)} collective-permute-done((f32[2,128,1024]{1,2,0:T(8,128)}, f32[2,128,1024]{1,2,0:T(8,128)S(1)}, u32[]{:S(2)}, u32[]{:S(2)}) %collective-permute-start.5) | collective-permute-done | bytes 1048608 | tf_op jit(solution)/shard_map/ppermute | solution.py:14
  708.0 20.2 %all-gather.25.cloned.1.call-done = f32[1024,1024]{0,1:T(8,128)} async-done(((f32[256,1024]{0,1:T(8,128)}), f32[1024,1024]{0,1:T(8,128)}) %all-gather.25.cloned.1.call-update) | async-done | bytes 4194320 | tf_op jit(solution)/shard_map/all_gather | solution.py:119
  843.6 39.3 %custom-call.56 = f32[4,128,128]{1,2,0:T(8,128)S(1)} custom-call(f32[4,128,128]{2,1,0:T(8,128)S(1)} %get-tuple-element.49), custom_call_target="InvertDiagBlocksLowerTriangular" | custom-call | tf_op jit(solution)/shard_map/triangular_solve/custom-call.3 | solution.py:23
  923.4 12.5 cholesky.884
  950.6 13.2 cholesky.905
  1001.4 23.2 %while.15 = (s32[]{:T(128)}, f32[1024,1024]{1,0:T(8,128)}, s32[8,2]{0,1:T(2,128)S(1)}, f32[8,128,128]{2,1,0:T(8,128)S(1)}, s32[]{:T(128)}) while((s32[]{:T(128)}, f32[1024,1024]{1,0:T(8,128)}, s32[8,2]{0,1:T(2,128)S(1)}, f32[8,128,128]{2,1,0:T(8,128)S(1)}, s32[]{:T(128)}) %tuple.291), condition=%wide.while_cond.1.clone, body=%wide.while_body.1.clone.sunk | while | flops 2 | bytes 131189 | solution.py:121
  1024.6 79.6 %custom-call.60 = f32[8,128,128]{1,2,0:T(8,128)} custom-call(f32[8,128,128]{2,1,0:T(8,128)S(1)} %get-tuple-element.50), custom_call_target="InvertDiagBlocksLowerTriangular" | custom-call | tf_op jit(solution)/shard_map/triangular_solve/custom-call.8 | solution.py:121
  1123.7 34.1 %all-gather.27.cloned.1.call-done = f32[512,1024]{0,1:T(8,128)} async-done(((f32[128,1024]{0,1:T(8,128)}), f32[512,1024]{0,1:T(8,128)}) %all-gather.27.cloned.1.call-update) | async-done | bytes 2097168 | tf_op jit(solution)/shard_map/all_gather | solution.py:132
  1176.2 23.4 %all-gather.31.cloned.1.call-done = f32[512,512]{0,1:T(8,128)} async-done(((f32[128,512]{0,1:T(8,128)}), f32[512,512]{0,1:T(8,128)}) %all-gather.31.cloned.1.call-update) | async-done | bytes 1048592 | tf_op jit(solution)/shard_map/all_gather | solution.py:112
  1206.0 21.9 %all-gather.29.cloned.1.call-done = f32[512,512]{0,1:T(8,128)} async-done(((f32[128,512]{0,1:T(8,128)}), f32[512,512]{0,1:T(8,128)}) %all-gather.29.cloned.1.call-update) | async-done | bytes 1048592 | tf_op jit(solution)/shard_map/all_gather | solution.py:111
  1263.9 34.7 %all-gather.33.cloned.1.call-done = f32[1024,1024]{0,1:T(8,128)} async-done(((f32[256,1024]{0,1:T(8,128)}), f32[1024,1024]{0,1:T(8,128)}) %all-gather.33.cloned.1.call-update) | async-done | bytes 4194320 | tf_op jit(solution)/shard_map/all_gather | solution.py:119
  1422.0 39.3 %custom-call.64 = f32[4,128,128]{1,2,0:T(8,128)S(1)} custom-call(f32[4,128,128]{2,1,0:T(8,128)S(1)} %get-tuple-element.51), custom_call_target="InvertDiagBlocksLowerTriangular" | custom-call | tf_op jit(solution)/shard_map/triangular_solve/custom-call.3 | solution.py:23
  1566.5 23.2 %while.17 = (s32[]{:T(128)}, f32[1024,1024]{1,0:T(8,128)}, s32[8,2]{0,1:T(2,128)S(1)}, f32[8,128,128]{2,1,0:T(8,128)S(1)}, s32[]{:T(128)}) while((s32[]{:T(128)}, f32[1024,1024]{1,0:T(8,128)}, s32[8,2]{0,1:T(2,128)S(1)}, f32[8,128,128]{2,1,0:T(8,128)S(1)}, s32[]{:T(128)}) %tuple.292), condition=%wide.while_cond.1.clone.1, body=%wide.while_body.1.clone.1.sunk | while | flops 2 | bytes 131189 | solution.py:121
  1589.7 78.8 %custom-call.68 = f32[8,128,128]{1,2,0:T(8,128)S(1)} custom-call(f32[8,128,128]{2,1,0:T(8,128)S(1)} %get-tuple-element.52), custom_call_target="InvertDiagBlocksLowerTriangular" | custom-call | tf_op jit(solution)/shard_map/triangular_solve/custom-call.8 | solution.py:121
  1693.6 21.7 %all-gather.35.cloned.1.call-done = f32[512,1024]{0,1:T(8,128)} async-done(((f32[128,1024]{0,1:T(8,128)}), f32[512,1024]{0,1:T(8,128)}) %all-gather.35.cloned.1.call-update) | async-done | bytes 2097168 | tf_op jit(solution)/shard_map/all_gather | solution.py:132
  (600 shorter events, 1001.1 us)
Async XLA Ops:
  7.2 30.1 %all-gather.15.cloned.1.call-start = ((), (), s32[]{:S(2)}) async-start(), calls=%async_computation.1 | async-start | bytes 1310720 | tf_op jit(solution)/shard_map/all_gather | solution.py:112
  7.2 2.9 collective-permute-start
  11.9 51.3 %all-gather.13.cloned.1.call-start = ((), (), s32[]{:S(2)}) async-start(), calls=%async_computation | async-start | bytes 1310720 | tf_op jit(solution)/shard_map/all_gather | solution.py:111
  15.5 58.0 %collective-permute-start.1 = (f32[3,256,1024]{1,2,0:T(8,128)}, f32[3,256,1024]{1,2,0:T(8,128)}, u32[]{:S(2)}, u32[]{:S(2)}) collective-permute-start(f32[3,256,1024]{1,2,0:T(8,128)} %bitcast.5), channel_id=1, source_target_pairs={{0,4},{4,0},{8,12},{12,8},{16,20},{20,16},{24,28},{28,24},{32,36},... | collective-permute-start | bytes 9437192 | tf_op jit(solution)/shard_map/ppermute | solution.py:14
  15.9 112.8 %all-gather.17.cloned.1.call-start = ((), (), s32[]{:S(2)}) async-start(), calls=%async_computation.2 | async-start | bytes 5242880 | tf_op jit(solution)/shard_map/all_gather | solution.py:119
  79.1 514.7 %all-gather.19.cloned.1.call-start = ((), (), s32[]{:S(2)}) async-start(), calls=%async_computation.3 | async-start | bytes 2621440 | tf_op jit(solution)/shard_map/all_gather | solution.py:132
  82.1 5.0 collective-permute-start.2
  559.7 97.2 %all-gather.23.cloned.1.call-start = ((), (), s32[]{:S(2)}) async-start(), calls=%async_computation.5 | async-start | bytes 1310720 | tf_op jit(solution)/shard_map/all_gather | solution.py:112
  599.0 6.4 collective-permute-start.3
  607.2 56.3 %all-gather.21.cloned.1.call-start = ((), (), s32[]{:S(2)}) async-start(), calls=%async_computation.4 | async-start | bytes 1310720 | tf_op jit(solution)/shard_map/all_gather | solution.py:111
  608.7 45.0 %collective-permute-start.4 = (f32[2,256,1024]{1,2,0:T(8,128)}, f32[2,256,1024]{1,2,0:T(8,128)}, u32[]{:S(2)}, u32[]{:S(2)}) collective-permute-start(f32[2,256,1024]{1,2,0:T(8,128)} %slice.559), channel_id=1, source_target_pairs={{0,8},{4,12},{8,0},{12,4},{16,24},{20,28},{24,16},{28,20},{32,40},... | collective-permute-start | bytes 6291464 | tf_op jit(solution)/shard_map/ppermute | solution.py:14
  610.0 118.3 %all-gather.25.cloned.1.call-start = ((), (), s32[]{:S(2)}) async-start(), calls=%async_computation.6 | async-start | bytes 5242880 | tf_op jit(solution)/shard_map/all_gather | solution.py:119
  678.0 479.8 %all-gather.27.cloned.1.call-start = ((), (), s32[]{:S(2)}) async-start(), calls=%async_computation.7 | async-start | bytes 2621440 | tf_op jit(solution)/shard_map/all_gather | solution.py:132
  680.3 23.4 %collective-permute-start.5 = (f32[2,128,1024]{1,2,0:T(8,128)}, f32[2,128,1024]{1,2,0:T(8,128)S(1)}, u32[]{:S(2)}, u32[]{:S(2)}) collective-permute-start(f32[2,128,1024]{1,2,0:T(8,128)} %slice.576), channel_id=1, source_target_pairs={{0,8},{4,12},{8,0},{12,4},{16,24},{20,28},{24,16},{28,20},{32,40},... | collective-permute-start | bytes 3145736 | tf_op jit(solution)/shard_map/ppermute | solution.py:14
  994.7 109.5 %copy-start.22 = (f32[128,1024]{0,1:T(8,128)S(1)}, f32[128,1024]{0,1:T(8,128)}, u32[]{:S(2)}) copy-start(f32[128,1024]{0,1:T(8,128)} %fusion.50) | copy-start | bytes 1572868
  1116.3 56.1 %copy-start.33 = (s32[384]{0:T(512)S(1)}, s32[384]{0:T(512)}, u32[]{:S(2)}) copy-start(s32[384]{0:T(512)} %get-tuple-element.59) | copy-start | bytes 4612
  1123.6 75.9 %all-gather.31.cloned.1.call-start = ((), (), s32[]{:S(2)}) async-start(), calls=%async_computation.9 | async-start | bytes 1310720 | tf_op jit(solution)/shard_map/all_gather | solution.py:112
  1162.9 7.8 collective-permute-start.6
  1171.6 56.3 %all-gather.29.cloned.1.call-start = ((), (), s32[]{:S(2)}) async-start(), calls=%async_computation.8 | async-start | bytes 1310720 | tf_op jit(solution)/shard_map/all_gather | solution.py:111
  1172.2 126.4 %all-gather.33.cloned.1.call-start = ((), (), s32[]{:S(2)}) async-start(), calls=%async_computation.10 | async-start | bytes 5242880 | tf_op jit(solution)/shard_map/all_gather | solution.py:119
  1173.4 72.2 %collective-permute-start.7 = (f32[1,256,1024]{1,2,0:T(8,128)}, f32[1,256,1024]{1,2,0:T(8,128)}, u32[]{:S(2)}, u32[]{:S(2)}) collective-permute-start(f32[1,256,1024]{1,2,0:T(8,128)} %slice.601), channel_id=1, source_target_pairs={{0,16},{4,20},{8,24},{12,28},{16,0},{20,4},{24,8},{28,12},{32,48},... | collective-permute-start | bytes 3145736 | tf_op jit(solution)/shard_map/ppermute | solution.py:14
  1248.4 466.9 %all-gather.35.cloned.1.call-start = ((), (), s32[]{:S(2)}) async-start(), calls=%async_computation.11 | async-start | bytes 2621440 | tf_op jit(solution)/shard_map/all_gather | solution.py:132
  1248.5 13.5 collective-permute-start.8
  1560.9 107.5 %copy-start.23 = (f32[128,1024]{0,1:T(8,128)S(1)}, f32[128,1024]{0,1:T(8,128)}, u32[]{:S(2)}) copy-start(f32[128,1024]{0,1:T(8,128)} %slice_add_fusion.1) | copy-start | bytes 1572868
  (48 other events, 634.0 us)
Sparse Core Ops, SparseCore 0:
  12.0 25.1 all-gather.14
  38.9 24.2 all-gather.12
  79.2 49.4 all-gather.16
  559.8 33.9 all-gather.18
  607.3 27.7 all-gather.22
  636.6 26.8 all-gather.20
  678.1 50.0 all-gather.24
  1123.7 33.9 all-gather.26
  1171.8 27.7 all-gather.30
  1201.0 26.8 all-gather.28
  1248.5 50.0 all-gather.32
  1681.2 33.9 all-gather.34
where the time goes:
time: 1740 us; the launch traced here: 1730 us
  other arithmetic  934 us (54%)
  waiting for transfers between devices  362 us (21%)
  local copies, waits for them, and re-layouts  221 us (13%)
  matrix products  163 us (9%)
  between operations  31.4 us (2%)
    another operation x90, other arithmetic, block_cholesky(): return jnp.linalg.cholesky(matrix, symmetrize_input=False)  494 us
    another operation x5, other arithmetic, on_device(): lax.linalg.triangular_solve(pivot_factor, front_below, left_side=False, l...  245 us
    another operation x7, other arithmetic, block_cholesky(): lax.linalg.triangular_solve(top_factor, matrix[half:, :half], left_side=F...  124 us
    all_gather x3, waiting for transfers between devices, on_device(): pivot_block = lax.all_gather(front_pivot, 'rows', axis=0, tiled=True)  91.3 us
    ppermute x9, waiting for transfers between devices, partner(): lax.ppermute(x, axis, [(i, i ^ 1 << stride) for i in range(lax.axis_size(...  90.8 us
    all_gather x3, waiting for transfers between devices, on_device(): lax.all_gather(solved, 'rows', axis=0, tiled=True)  89.8 us
    another operation x76, local copies, waits for them, and re-layouts, on_device(): lax.linalg.triangular_solve(pivot_factor, front_below, left_side=False, l...  75.5 us
    another operation x45, matrix products, on_device(): lax.linalg.triangular_solve(pivot_factor, front_below, left_side=False, l...  53.7 us
  transfers between devices with their start and end apart: 21, of which 18 were waited for; matrix products, arithmetic and copies ran while one was open for 5% of the time, Pallas kernels for 0%

commit v1 on v0

v1 whole, which is shorter than its diff:
```python
import jax
import jax.numpy as jnp
from jax import lax
from jax.experimental import pallas as pl
from jax.experimental.pallas import tpu as pltpu
from jax.sharding import PartitionSpec as P

BLK = 128
SEP = 1024
UPD = 512
FRONT = SEP + UPD
LEVELS = 3
NSEP = SEP // BLK
NUPD = UPD // BLK
f32 = jnp.float32
bf16 = jnp.bfloat16


def lane_b(x, c):
    return jnp.broadcast_to(x[:, c : c + 1], x.shape)


def sub_b(x, i):
    return jnp.broadcast_to(x[i : i + 1, :], x.shape)


def block_inverse(rows_a):
    groups = BLK // 8
    row = lax.broadcasted_iota(jnp.int32, (8, BLK), 0)
    col = lax.broadcasted_iota(jnp.int32, (8, BLK), 1)
    A = list(rows_a)
    V = [jnp.where(col == row + 8 * g, 1.0, 0.0).astype(f32) for g in range(groups)]
    out = []
    for b in range(groups):
        c0 = 8 * b
        cols = [lane_b(A[b], c0 + j) for j in range(8)]
        d = [[sub_b(cols[j], i) if i >= j else None for j in range(8)] for i in range(8)]
        xs = [sub_b(A[b], i) for i in range(8)]
        ys = [sub_b(V[b], i) for i in range(8)]
        rs = []
        for k in range(8):
            r = lax.rsqrt(d[k][k])
            rs.append(r)
            for i in range(k + 1, 8):
                d[i][k] = d[i][k] * r
            for j in range(k + 1, 8):
                for i in range(j, 8):
                    d[i][j] = d[i][j] - d[i][k] * d[j][k]
            xs[k] = xs[k] * r
            ys[k] = ys[k] * r
            for i in range(k + 1, 8):
                xs[i] = xs[i] - d[i][k] * xs[k]
                ys[i] = ys[i] - d[i][k] * ys[k]
        for g in range(b + 1, groups):
            cg = [lane_b(A[g], c0 + j) for j in range(8)]
            for k in range(8):
                cg[k] = cg[k] * rs[k]
                for i in range(k + 1, 8):
                    cg[i] = cg[i] - d[i][k] * cg[k]
            for k in range(8):
                A[g] = A[g] - cg[k] * xs[k]
                V[g] = V[g] - cg[k] * ys[k]
        y = ys[0]
        for k in range(1, 8):
            y = jnp.where(row == k, ys[k], y)
        out.append(y)
    return out


def split(x):
    hi = x.astype(bf16)
    return hi, (x - hi.astype(f32)).astype(bf16)


def nt(a, b):
    return lax.dot_general(a, b, (((1,), (1,)), ((), ())), preferred_element_type=f32)


def nt3(a_hi, a_lo, b_hi, b_lo):
    return nt(a_hi, b_hi) + (nt(a_hi, b_lo) + nt(a_lo, b_hi))


def blk(i):
    if isinstance(i, int):
        return pl.ds(i * BLK, BLK)
    return pl.ds(pl.multiple_of(i * BLK, BLK), BLK)


def front_body(level, refs):
    if level == 0:
        ids, sep_in, cpl_in, u_in = refs[:4]
        refs = refs[4:]
    else:
        ids, sep_in, cpl_in, own_in, near_in, far_in = refs[:6]
        refs = refs[6:]
    l_out, r_out, u_out, F, C, Ub, Lh, Ll, Lf, T, D, E, Wh, Wl, sem = refs
    rid = ids[8]
    half = ids[9]
    leaves = 2 << level
    sep_piece = 256 // leaves
    cpl_piece = 128 // leaves
    copies = []
    for leaf in range(leaves):
        slot = 0
        for bit in range(level + 1):
            slot += (leaf >> bit & 1) * (leaves >> bit + 1)
        for r in range(4):
            copies.append((sep_in.at[leaf, r], F.at[pl.ds(r * 256 + slot * sep_piece, sep_piece), :]))
            copies.append((cpl_in.at[leaf, r], F.at[pl.ds(SEP + r * BLK + slot * cpl_piece, cpl_piece), :]))
    if level == 0:
        copies.append((u_in, Ub))
    else:
        copies.append((own_in, Ub.at[0]))
        copies.append((near_in, Ub.at[1, pl.ds(pl.multiple_of(half * 256, 256), 256), :]))
        copies.append((far_in, Ub.at[1, pl.ds(pl.multiple_of((1 - half) * 256, 256), 256), :]))
    copies = [pltpu.make_async_copy(s, t, sem.at[n]) for n, (s, t) in enumerate(copies)]
    for c in copies:
        c.start()
    C[...] = jnp.zeros_like(C)
    Lh[...] = jnp.zeros_like(Lh)
    Ll[...] = jnp.zeros_like(Ll)
    for c in copies:
        c.wait()

    def add_block(t, c):
        child = t // 16
        i = t // 4 % 4
        j = t % 4
        mi = ids[4 * child + i]
        mj = ids[4 * child + j]
        part = Ub[child, blk(i), blk(j)]

        @pl.when(mj < NSEP)
        def _():
            F[blk(mi), blk(mj)] += part

        @pl.when((mj >= NSEP) & (mi >= NSEP))
        def _():
            C[blk(jnp.maximum(mi - NSEP, 0)), blk(jnp.maximum(mj - NSEP, 0))] += part

        return c

    lax.fori_loop(0, 32, add_block, 0)
    D[...] = F[:BLK, :BLK]

    def panel(k, lo):
        th, tl = split(T[lo:, :])
        v = nt3(th, tl, Wh[...], Wl[...])
        Lf[lo:, blk(k)] = v
        h, l = split(v)
        Lh[lo:, blk(k)] = h
        Ll[lo:, blk(k)] = l

    def step(k, lo, depth):
        if depth == 0:
            n = 1
            T[...] = F[:, :BLK]
            E[...] = F[blk(1), blk(1)]
        else:
            n = jnp.minimum(k + 1, NSEP - 1)
            panel(k - 1, lo)
            T[lo:, :] = F[lo:, blk(k)] - nt3(
                Lh[lo:, :depth], Ll[lo:, :depth], Lh[blk(k), :depth], Ll[blk(k), :depth]
            )
            nh = Lh[blk(n), :depth]
            nl = Ll[blk(n), :depth]
            E[...] = F[blk(n), blk(n)] - nt3(nh, nl, nh, nl)
        W = jnp.concatenate(block_inverse([D[8 * g : 8 * g + 8, :] for g in range(BLK // 8)]), axis=0)
        wh, wl = split(W)
        Wh[...] = wh
        Wl[...] = wl
        th, tl = split(T[blk(n), :])
        h, l = split(nt3(th, tl, wh, wl))
        D[...] = E[...] - nt3(h, l, h, l)

    step(0, 0, 0)
    lax.fori_loop(1, 4, lambda k, c: (step(k, 0, 512), c)[1], 0)
    lax.fori_loop(4, 8, lambda k, c: (step(k, 384, 1024), c)[1], 0)
    panel(7, 896)
    rh = Lh[SEP:, :]
    rl = Ll[SEP:, :]
    if level == LEVELS - 1:
        mine = pl.ds(pl.multiple_of(rid * BLK, BLK), BLK)
        mine_l = pl.ds(pl.multiple_of(SEP + rid * BLK, BLK), BLK)
        u_out[...] = C[mine, :] - nt3(Lh[mine_l, :], Ll[mine_l, :], rh, rl)
    else:
        u_out[...] = C[...] - nt3(rh, rl, rh, rl)
    rows = pl.ds(pl.multiple_of(rid * 256, 256), 256)
    ri = lax.broadcasted_iota(jnp.int32, (256, SEP), 0) + rid * 256
    ci = lax.broadcasted_iota(jnp.int32, (256, SEP), 1)
    l_out[...] = jnp.where(ri >= ci, Lf[rows, :], 0.0)
    r_out[...] = Lf[pl.ds(pl.multiple_of(SEP + rid * BLK, BLK), BLK), :]


def front(level, ids, sep_in, cpl_in, *updates):
    smem = pl.BlockSpec(memory_space=pltpu.SMEM)
    vmem = pl.BlockSpec(memory_space=pltpu.VMEM)
    hbm = pl.BlockSpec(memory_space=pl.ANY)
    last = level == LEVELS - 1
    copies = 2 * 4 * (2 << level) + 3
    return pl.pallas_call(
        lambda *refs: front_body(level, refs),
        in_specs=[smem] + [hbm] * (2 + len(updates)),
        out_specs=[vmem] * 3,
        out_shape=[
            jax.ShapeDtypeStruct((256, SEP), f32),
            jax.ShapeDtypeStruct((BLK, SEP), f32),
            jax.ShapeDtypeStruct((BLK if last else UPD, UPD), f32),
        ],
        scratch_shapes=[
            pltpu.VMEM((FRONT, SEP), f32),
            pltpu.VMEM((UPD, UPD), f32),
            pltpu.VMEM((2, UPD, UPD), f32),
            pltpu.VMEM((FRONT, SEP), bf16),
            pltpu.VMEM((FRONT, SEP), bf16),
            pltpu.VMEM((FRONT, SEP), f32),
            pltpu.VMEM((FRONT, BLK), f32),
            pltpu.VMEM((BLK, BLK), f32),
            pltpu.VMEM((BLK, BLK), f32),
            pltpu.VMEM((BLK, BLK), bf16),
            pltpu.VMEM((BLK, BLK), bf16),
            pltpu.SemaphoreType.DMA((copies,)),
        ],
        compiler_params=pltpu.CompilerParams(vmem_limit_bytes=48 << 20),
        cost_estimate=pl.CostEstimate(flops=20_000_000_000, transcendentals=0, bytes_accessed=20_000_000),
        name=f"front{level}",
    )(ids, sep_in, cpl_in, *updates)


def swap(x, stride):
    return lax.ppermute(x, "leaf", [(i, i ^ 1 << stride) for i in range(lax.axis_size("leaf"))])


def gather_group(x, level):
    leaves = 2 << level
    groups = [
        [(g * leaves + l) * 4 + r for l in range(leaves) for r in range(4)]
        for g in range(lax.axis_size("leaf") // leaves)
    ]
    return lax.all_gather(x, ("leaf", "rows"), axis_index_groups=groups, axis=0, tiled=False)


def scatter_sum(x, stride, bit):
    half = x.shape[0] // 2
    halves = x.reshape(2, half, x.shape[1])
    keep = lax.dynamic_index_in_dim(halves, bit, 0, keepdims=False)
    give = lax.dynamic_index_in_dim(halves, 1 - bit, 0, keepdims=False)
    return keep + swap(give, stride)


def on_device(child_update, block_maps, sep_share, coupling_share):
    leaf = lax.axis_index("leaf")
    rid = lax.axis_index("rows")
    bits = [leaf >> b & 1 for b in range(LEVELS)]
    seps = []
    cpls = []
    for level in range(LEVELS):
        s = sep_share[0, level]
        c = coupling_share[0, level]
        for b in range(level + 1):
            s = scatter_sum(s, b, bits[b])
            c = scatter_sum(c, b, bits[b])
        s, c = gather_group(s, level), gather_group(c, level)
        seps.append(s.reshape(2 << level, 4, s.shape[1], SEP))
        cpls.append(c.reshape(2 << level, 4, c.shape[1], SEP))
    children = gather_group(child_update[0], 0).reshape(2, UPD, UPD)
    diag_parts = []
    below_parts = []
    current = None
    for level in range(LEVELS):
        if level == 0:
            first = (leaf >> 1) * 2
            child_ids = (first, first + 1)
            updates = (children,)
        else:
            own = leaf >> level
            child_ids = (own, own ^ 1)
            give = lax.dynamic_index_in_dim(current.reshape(2, 256, UPD), bits[0], 0, keepdims=False)
            near = swap(give, level)
            far = swap(near, 0)
            updates = (current, near, far)
        ids = jnp.concatenate(
            [lax.dynamic_index_in_dim(block_maps[level], i, 0, keepdims=False) for i in child_ids]
            + [jnp.stack([rid, bits[0]]).astype(jnp.int32)]
        )
        l_rows, r_rows, current = front(level, ids, seps[level], cpls[level], *updates)
        diag_parts.append(l_rows)
        below_parts.append(r_rows)
    return (jnp.stack(diag_parts)[None], jnp.stack(below_parts)[None], current[None])


def solution(mesh):
    return jax.shard_map(
        on_device,
        mesh=mesh,
        in_specs=(
            P("leaf", "rows", None),
            P(),
            P("leaf", None, "rows", None),
            P("leaf", None, "rows", None),
        ),
        out_specs=(
            P("leaf", None, "rows", None),
            P("leaf", None, "rows", None),
            P("leaf", "rows", None),
        ),
        check_vma=False,
    )
```

time: 1740 us -> 371 us (0.21)
  other arithmetic: 934 us -> 8.98 us
  waiting for transfers between devices: 362 us -> 148 us
  local copies, waits for them, and re-layouts: 221 us -> 13.1 us
  matrix products: 163 us -> 0 us
  Pallas kernels: 0 us -> 155 us
    another operation x102 -> x0, other arithmetic: 863 us -> none  [the longest x90 494 us: block_cholesky(): return jnp.linalg.cholesky(matrix, symmetrize_input=False)]
    all_gather x12 -> x7, waiting for transfers between devices: 271 us -> 89 us  [gather_group(): lax.all_gather(x, ('leaf', 'rows'), axis_index_groups=groups, axis=0, til...]
    pallas_call x0 -> x3, Pallas kernels: none -> 155 us  [front(): pl.pallas_call(lambda *refs: front_body(level, refs), in_specs=[smem] + [...]
    another operation x166 -> x0, local copies, waits for them, and re-layouts: 135 us -> none  [the longest x76 75.5 us: on_device(): lax.linalg.triangular_solve(pivot_factor, front_below, left_side=False, l...]
    another operation x102 -> x0, matrix products: 123 us -> none  [the longest x45 53.7 us: on_device(): lax.linalg.triangular_solve(pivot_factor, front_below, left_side=False, l...]
    dot_general x12 -> x0, matrix products: 40 us -> none  [the longest x3 15.3 us: product(): jnp.dot(left_part, portion.T, precision=highest, preferred_element_type=j...]
    ppermute x9 -> x16, waiting for transfers between devices: 90.8 us -> 57.9 us  [swap(): lax.ppermute(x, 'leaf', [(i, i ^ 1 << stride) for i in range(lax.axis_siz...]
    add x13 -> x12, other arithmetic: 30 us -> 5.54 us  [scatter_sum(): return keep + swap(give, stride)]
  transfers between devices with their start and end apart: 21 -> 23, of which waited for: 18 -> 17; matrix products, arithmetic and copies ran while one was open for 5% -> 3% of each run, Pallas kernels for 0% -> 28%
where the time goes in v1:
time: 371 us; the launch traced here: 366 us
  Pallas kernels  155 us (42%)
  waiting for transfers between devices  148 us (40%)
  starting transfers between devices  27.7 us (7%)
  between operations  14.6 us (4%)
  local copies, waits for them, and re-layouts  13.1 us (4%)
  other arithmetic  8.98 us (2%)
    pallas_call x3, Pallas kernels, front(): pl.pallas_call(lambda *refs: front_body(level, refs), in_specs=[smem] + [...  155 us
    all_gather x7, waiting for transfers between devices, gather_group(): lax.all_gather(x, ('leaf', 'rows'), axis_index_groups=groups, axis=0, til...  89 us
    ppermute x16, waiting for transfers between devices, swap(): lax.ppermute(x, 'leaf', [(i, i ^ 1 << stride) for i in range(lax.axis_siz...  57.9 us
    ppermute x16, starting transfers between devices, swap(): lax.ppermute(x, 'leaf', [(i, i ^ 1 << stride) for i in range(lax.axis_siz...  27.4 us
    unnamed x18, local copies, waits for them, and re-layouts  8.44 us
  transfers between devices with their start and end apart: 23, of which 17 were waited for; matrix products, arithmetic and copies ran while one was open for 3% of the time, Pallas kernels for 28%

profile of v1, /device:TPU:1, one launch (start us, length us, event | category | flops | bytes accessed | tf_op | source)
XLA Modules:
  0.0 366.5 jit_solution(15178128655685523863)
XLA Ops:
  12.9 2.1 fusion.6
  22.3 3.3 collective-permute-done.5
  30.8 6.2 %collective-permute-done.3 = f32[64,1024]{1,0:T(8,128)S(1)} collective-permute-done((f32[64,1024]{1,0:T(8,128)S(1)}, f32[64,1024]{1,0:T(8,128)S(1)}, u32[]{:S(2)}, u32[]{:S(2)}) %collective-permute-start.3) | collective-permute-done | bytes 262176 | tf_op jit(solution)/shard_map/ppermute | solution.py:231
  41.7 3.3 collective-permute-done.12
  45.1 3.1 collective-permute-start.13
  48.2 1.7 collective-permute-done.13
  50.6 2.4 collective-permute-start.8
  56.1 6.2 %collective-permute-done.9 = f32[64,1024]{1,0:T(8,128)S(1)} collective-permute-done((f32[64,1024]{1,0:T(8,128)S(1)}, f32[64,1024]{1,0:T(8,128)S(1)}, u32[]{:S(2)}, u32[]{:S(2)}) %collective-permute-start.9) | collective-permute-done | bytes 262176 | tf_op jit(solution)/shard_map/ppermute | solution.py:231
  62.4 3.6 collective-permute-start.10
  66.0 2.4 collective-permute-done.10
  69.4 31.6 %all-gather.16.cloned.1.call-done = f32[1024,1024]{1,0:T(8,128)} async-done(((f32[128,1024]{1,0:T(8,128)}), f32[1024,1024]{1,0:T(8,128)}) %all-gather.16.cloned.1.call-update) | async-done | bytes 4194320 | tf_op jit(solution)/shard_map/all_gather | solution.py:240
  101.0 1.6 copy-done.4
  102.6 50.7 %front0.1 = (f32[256,1024]{1,0:T(8,128)S(1)}, f32[128,1024]{1,0:T(8,128)S(1)}, f32[512,512]{1,0:T(8,128)S(1)}) custom-call(s32[10]{0:T(128)S(1)} %add_add_fusion.refs_0_, f32[2,4,128,1024]{3,2,1,0:T(8,128)} %bitcast.120, f32[2,4,64,1024]{3,2,1,0:T(8,128)S(1)} %bitcast.94, f32[2,512,512]{2,1,0:T(8,128)} %bitcast.123), custom_call_target="tpu_custom_call" | custom-call | flops 20000000000 | bytes 20000000 | tf_op jit(solution)/shard_map/front0/pallas_call | solution.py:201
  154.5 13.4 %collective-permute-done.6.refs_4_ = f32[256,512]{1,0:T(8,128)S(1)} collective-permute-done((f32[256,512]{1,0:T(8,128)S(1)}, f32[256,512]{1,0:T(8,128)S(1)}, u32[]{:S(2)}, u32[]{:S(2)}) %collective-permute-start.6) | collective-permute-done | bytes 524320 | tf_op jit(solution)/shard_map/ppermute | solution.py:231
  167.9 1.6 collective-permute-start.7
  170.7 34.5 %all-gather.20.cloned.1.call-done = f32[1024,1024]{1,0:T(8,128)} async-done(((f32[64,1024]{1,0:T(8,128)}), f32[1024,1024]{1,0:T(8,128)}) %all-gather.20.cloned.1.call-update) | async-done | bytes 4194320 | tf_op jit(solution)/shard_map/all_gather | solution.py:240
  207.4 50.9 %front1.1 = (f32[256,1024]{1,0:T(8,128)S(1)}, f32[128,1024]{1,0:T(8,128)S(1)}, f32[512,512]{1,0:T(8,128)S(1)}) custom-call(s32[10]{0:T(128)S(1)} %add_add_fusion.1.refs_0_, f32[4,4,64,1024]{3,2,1,0:T(8,128)} %bitcast.121, f32[4,4,32,1024]{3,2,1,0:T(8,128)} %bitcast.124, f32[512,512]{1,0:T(8,128)S(1)} %copy-done.3, f32[256,512]{1,0:T(8,128)S(1)} %copy-done.7, ...), custom_call_target="tpu_custom_call" | custom-call | flops 20000000000 | bytes 20000000 | tf_op jit(solution)/shard_map/front1/pallas_call | solution.py:201
  259.4 2.5 collective-permute-start.14
  261.8 13.1 %collective-permute-done.14.refs_4_ = f32[256,512]{1,0:T(8,128)} collective-permute-done((f32[256,512]{1,0:T(8,128)S(1)}, f32[256,512]{1,0:T(8,128)}, u32[]{:S(2)}, u32[]{:S(2)}) %collective-permute-start.14) | collective-permute-done | bytes 524320 | tf_op jit(solution)/shard_map/ppermute | solution.py:231
  274.9 2.3 collective-permute-start.15
  277.6 22.9 %all-gather.24.cloned.1.call-done = f32[1024,1024]{1,0:T(8,128)} async-done(((f32[32,1024]{1,0:T(8,128)}), f32[1024,1024]{1,0:T(8,128)}) %all-gather.24.cloned.1.call-update) | async-done | bytes 4194320 | tf_op jit(solution)/shard_map/all_gather | solution.py:240
  301.7 1.6 copy-done.5
  303.3 52.9 %front2.1 = (f32[256,1024]{1,0:T(8,128)S(1)}, f32[128,1024]{1,0:T(8,128)S(1)}, f32[128,512]{1,0:T(8,128)}) custom-call(s32[10]{0:T(128)S(1)} %add_add_fusion.2.refs_0_, f32[8,4,32,1024]{3,2,1,0:T(8,128)} %bitcast.122, f32[8,4,16,1024]{3,2,1,0:T(8,128)S(1)} %bitcast.95, f32[512,512]{1,0:T(8,128)S(1)} %copy-done.1, ...), custom_call_target="tpu_custom_call" | custom-call | flops 20000000000 | bytes 20000000 | tf_op jit(solution)/shard_map/front2/pallas_call | solution.py:201
  357.5 1.9 maximum_bitcast_fusion
  (87 shorter events, 36.0 us)
Async XLA Ops:
  7.2 62.3 %all-gather.14.cloned.1.call-start = ((), (), s32[]{:S(2)}) async-start(), calls=%async_computation | async-start | bytes 2359296 | tf_op jit(solution)/shard_map/all_gather | solution.py:240
  7.9 61.5 %all-gather.18.cloned.1.call-start = ((), (), s32[]{:S(2)}) async-start(), calls=%async_computation.2 | async-start | bytes 2359296 | tf_op jit(solution)/shard_map/all_gather | solution.py:240
  9.5 2.7 collective-permute-start.1
  12.9 88.1 %all-gather.16.cloned.1.call-start = ((), (), s32[]{:S(2)}) async-start(), calls=%async_computation.1 | async-start | bytes 4718592 | tf_op jit(solution)/shard_map/all_gather | solution.py:240
  15.1 2.0 collective-permute-start
  18.0 152.7 %all-gather.22.cloned.1.call-start = ((), (), s32[]{:S(2)}) async-start(), calls=%async_computation.4 | async-start | bytes 2228224 | tf_op jit(solution)/shard_map/all_gather | solution.py:240
  18.0 1.7 collective-permute-start.4
  20.8 4.8 %collective-permute-start.5 = (f32[32,1024]{1,0:T(8,128)S(1)}, f32[32,1024]{1,0:T(8,128)S(1)}, u32[]{:S(2)}, u32[]{:S(2)}) collective-permute-start(f32[32,1024]{1,0:T(8,128)S(1)} %dynamic-slice_bitcast_fusion.12), channel_id=1, source_target_pairs={{0,8},{4,12},{8,0},{12,4},{16,24},{20,28},{24,16},{28,20},{32,40},... | collective-permute-start | bytes 393224 | tf_op jit(solution)/shard_map/ppermute | solution.py:231
  26.3 178.8 %all-gather.20.cloned.1.call-start = ((), (), s32[]{:S(2)}) async-start(), calls=%async_computation.3 | async-start | bytes 4456448 | tf_op jit(solution)/shard_map/all_gather | solution.py:240
  26.4 2.8 collective-permute-start.2
  29.3 7.7 %collective-permute-start.3 = (f32[64,1024]{1,0:T(8,128)S(1)}, f32[64,1024]{1,0:T(8,128)S(1)}, u32[]{:S(2)}, u32[]{:S(2)}) collective-permute-start(f32[64,1024]{1,0:T(8,128)S(1)} %dynamic-slice_bitcast_fusion.8), channel_id=1, source_target_pairs={{0,8},{4,12},{8,0},{12,4},{16,24},{20,28},{24,16},{28,20},{32,40},... | collective-permute-start | bytes 786440 | tf_op jit(solution)/shard_map/ppermute | solution.py:231
  37.8 239.8 %all-gather.26.cloned.1.call-start = ((), (), s32[]{:S(2)}) async-start(), calls=%async_computation.6 | async-start | bytes 2162688 | tf_op jit(solution)/shard_map/all_gather | solution.py:240
  37.9 2.4 collective-permute-start.11
  40.3 4.8 %collective-permute-start.12 = (f32[32,1024]{1,0:T(8,128)S(1)}, f32[32,1024]{1,0:T(8,128)S(1)}, u32[]{:S(2)}, u32[]{:S(2)}) collective-permute-start(f32[32,1024]{1,0:T(8,128)S(1)} %dynamic-slice_bitcast_fusion.10), channel_id=1, source_target_pairs={{0,8},{4,12},{8,0},{12,4},{16,24},{20,28},{24,16},{28,20},{32,40},... | collective-permute-start | bytes 393224 | tf_op jit(solution)/shard_map/ppermute | solution.py:231
  45.1 4.7 %collective-permute-start.13 = (f32[16,1024]{1,0:T(8,128)S(1)}, f32[16,1024]{1,0:T(8,128)S(1)}, u32[]{:S(2)}, u32[]{:S(2)}) collective-permute-start(f32[16,1024]{1,0:T(8,128)S(1)} %dynamic-slice_bitcast_fusion.13), channel_id=1, source_target_pairs={{0,16},{4,20},{8,24},{12,28},{16,0},{20,4},{24,8},{28,12},{32,48},... | collective-permute-start | bytes 196616 | tf_op jit(solution)/shard_map/ppermute | solution.py:231
  50.5 250.0 %all-gather.24.cloned.1.call-start = ((), (), s32[]{:S(2)}) async-start(), calls=%async_computation.5 | async-start | bytes 4325376 | tf_op jit(solution)/shard_map/all_gather | solution.py:240
  50.6 3.9 %collective-permute-start.8 = (f32[128,1024]{1,0:T(8,128)S(1)}, f32[128,1024]{1,0:T(8,128)S(1)}, u32[]{:S(2)}, u32[]{:S(2)}) collective-permute-start(f32[128,1024]{1,0:T(8,128)S(1)} %dynamic-slice_bitcast_fusion.1), channel_id=1, source_target_pairs={{0,4},{4,0},{8,12},{12,8},{16,20},{20,16},{24,28},{28,24},{32,36},... | collective-permute-start | bytes 1572872 | tf_op jit(solution)/shard_map/ppermute | solution.py:231
  54.7 7.7 %collective-permute-start.9 = (f32[64,1024]{1,0:T(8,128)S(1)}, f32[64,1024]{1,0:T(8,128)S(1)}, u32[]{:S(2)}, u32[]{:S(2)}) collective-permute-start(f32[64,1024]{1,0:T(8,128)S(1)} %dynamic-slice_bitcast_fusion.6), channel_id=1, source_target_pairs={{0,8},{4,12},{8,0},{12,4},{16,24},{20,28},{24,16},{28,20},{32,40},... | collective-permute-start | bytes 786440 | tf_op jit(solution)/shard_map/ppermute | solution.py:231
  62.4 6.0 %collective-permute-start.10 = (f32[32,1024]{1,0:T(8,128)S(1)}, f32[32,1024]{1,0:T(8,128)S(1)}, u32[]{:S(2)}, u32[]{:S(2)}) collective-permute-start(f32[32,1024]{1,0:T(8,128)S(1)} %dynamic-slice_bitcast_fusion.11), channel_id=1, source_target_pairs={{0,16},{4,20},{8,24},{12,28},{16,0},{20,4},{24,8},{28,12},{32,48},... | collective-permute-start | bytes 393224 | tf_op jit(solution)/shard_map/ppermute | solution.py:231
  153.2 51.9 %copy-start.2 = (f32[512,512]{1,0:T(8,128)}, f32[512,512]{1,0:T(8,128)S(1)}, u32[]{:S(2)}) copy-start(f32[512,512]{1,0:T(8,128)S(1)} %get-tuple-element.13.refs_3_) | copy-start | bytes 3145732
  153.3 14.6 %collective-permute-start.6 = (f32[256,512]{1,0:T(8,128)S(1)}, f32[256,512]{1,0:T(8,128)S(1)}, u32[]{:S(2)}, u32[]{:S(2)}) collective-permute-start(f32[256,512]{1,0:T(8,128)S(1)} %dynamic-slice_bitcast_fusion.2), channel_id=1, source_target_pairs={{0,8},{4,12},{8,0},{12,4},{16,24},{20,28},{24,16},{28,20},{32,40},... | collective-permute-start | bytes 1572872 | tf_op jit(solution)/shard_map/ppermute | solution.py:231
  167.9 37.2 %collective-permute-start.7 = (f32[256,512]{1,0:T(8,128)S(1)}, f32[256,512]{1,0:T(8,128)}, u32[]{:S(2)}, u32[]{:S(2)}) collective-permute-start(f32[256,512]{1,0:T(8,128)S(1)} %collective-permute-done.6.refs_4_), channel_id=1, source_target_pairs={{0,4},{4,0},{8,12},{12,8},{16,20},{20,16},{24,28},{28,24},{32,36},... | collective-permute-start | bytes 1572872 | tf_op jit(solution)/shard_map/ppermute | solution.py:231
  259.4 15.6 %collective-permute-start.14 = (f32[256,512]{1,0:T(8,128)S(1)}, f32[256,512]{1,0:T(8,128)}, u32[]{:S(2)}, u32[]{:S(2)}) collective-permute-start(f32[256,512]{1,0:T(8,128)S(1)} %dynamic-slice_bitcast_fusion), channel_id=1, source_target_pairs={{0,16},{4,20},{8,24},{12,28},{16,0},{20,4},{24,8},{28,12},{32,48},... | collective-permute-start | bytes 1572872 | tf_op jit(solution)/shard_map/ppermute | solution.py:231
  274.9 25.6 %collective-permute-start.15 = (f32[256,512]{1,0:T(8,128)}, f32[256,512]{1,0:T(8,128)}, u32[]{:S(2)}, u32[]{:S(2)}) collective-permute-start(f32[256,512]{1,0:T(8,128)} %collective-permute-done.14.refs_4_), channel_id=1, source_target_pairs={{0,4},{4,0},{8,12},{12,8},{16,20},{20,16},{24,28},{28,24},{32,36},... | collective-permute-start | bytes 1572872 | tf_op jit(solution)/shard_map/ppermute | solution.py:231
  (8 other events, 26.9 us)
Sparse Core Ops, SparseCore 0:
  9.7 28.7 all-gather.13
  40.8 25.3 all-gather.17
  68.6 32.3 all-gather.15
  102.5 46.9 all-gather.21
  151.6 53.5 all-gather.19
  207.2 44.1 all-gather.25
  253.7 46.7 all-gather.23

commit v2 on v1

v2 whole, which is shorter than its diff:
```python
import jax
import jax.numpy as jnp
from jax import lax
from jax.experimental import pallas as pl
from jax.experimental.pallas import tpu as pltpu
from jax.sharding import PartitionSpec as P

BLK = 128
SEP = 1024
UPD = 512
FRONT = SEP + UPD
LEVELS = 3
NSEP = SEP // BLK
PART = 8
f32 = jnp.float32
bf16 = jnp.bfloat16


def lane_b(x, c):
    return jnp.broadcast_to(x[:, c : c + 1], x.shape)


def sub_b(x, i):
    return jnp.broadcast_to(x[i : i + 1, :], x.shape)


def block_inverse(rows_a):
    groups = BLK // 8
    row = lax.broadcasted_iota(jnp.int32, (8, BLK), 0)
    lane = lax.broadcasted_iota(jnp.int32, (8, BLK), 1)
    M = list(rows_a)
    out = []
    for s in range(0, groups, PART):
        e = s + PART
        cols = [lane_b(M[s], 8 * s + j) for j in range(8)]
        zrows = []
        for b in range(s, e):
            c0 = 8 * b
            inside = (lane >= c0) & (lane < c0 + 8)
            coef = {g: [lane_b(M[g], c0 + k) for k in range(8)] for g in range(b + 1, e)}
            following = [lane_b(M[b + 1], c0 + 8 + j) for j in range(8)] if b + 1 < e else None
            X = jnp.where(inside, jnp.where(lane - c0 == row, 1.0, 0.0), M[b])
            rs = []
            zs = []
            ls = [[None] * 8 for _ in range(8)]
            pivot = sub_b(cols[0], 0)
            for k in range(8):
                r = lax.rsqrt(pivot)
                rs.append(r)
                if k < 7:
                    below = sub_b(cols[k], k + 1) * r
                    pivot = sub_b(cols[k + 1], k + 1) - below * below
                c = cols[k] * r
                for j in range(k + 1, 8):
                    ls[j][k] = sub_b(c, j)
                    cols[j] = cols[j] - c * ls[j][k]
                z = sub_b(X, k) * r
                zs.append(z)
                if k < 7:
                    X = X - jnp.where(row > k, c, 0.0) * z
            for g in range(b + 1, e):
                cg = coef[g]
                for k in range(8):
                    cg[k] = cg[k] * rs[k]
                    for i in range(k + 1, 8):
                        cg[i] = cg[i] - ls[i][k] * cg[k]
                m = jnp.where(inside, 0.0, M[g])
                for k in range(8):
                    m = m - cg[k] * zs[k]
                M[g] = m
                if g == b + 1:
                    for k in range(8):
                        for j in range(8):
                            following[j] = following[j] - cg[k] * sub_b(cg[k], j)
                    cols = following
            y = zs[0]
            for k in range(1, 8):
                y = jnp.where(row == k, zs[k], y)
            zrows.append(jnp.where((lane < c0 + 8) | (lane >= 8 * e), y, 0.0))
            out.append(jnp.where(lane < c0 + 8, y, 0.0))
        if e < groups:
            zh, zl = split(jnp.concatenate(zrows, axis=0))
            lhs = jnp.concatenate([zh, zh, zl], axis=0)[:, 8 * e :]
            rhs = jnp.concatenate([zh, zl, zh], axis=0)
            upd = lax.dot_general(lhs, rhs, (((0,), (0,)), ((), ())), preferred_element_type=f32)
            done = (lane >= 8 * s) & (lane < 8 * e)
            for g in range(e, groups):
                M[g] = jnp.where(done, 0.0, M[g]) - upd[8 * (g - e) : 8 * (g - e) + 8, :]
    return out


def split(x):
    hi = x.astype(bf16)
    return hi, (x - hi.astype(f32)).astype(bf16)


def nt(a, b):
    return lax.dot_general(a, b, (((1,), (1,)), ((), ())), preferred_element_type=f32)


def nt3(a_hi, a_lo, b_hi, b_lo):
    return nt(a_hi, b_hi) + (nt(a_hi, b_lo) + nt(a_lo, b_hi))


def blk(i):
    if isinstance(i, int):
        return pl.ds(i * BLK, BLK)
    return pl.ds(pl.multiple_of(i * BLK, BLK), BLK)


def front_body(level, refs):
    ids, mine, theirs = refs[:3]
    if level == 0:
        refs = refs[3:]
    else:
        own_in, near_in, far_in = refs[3:6]
        refs = refs[6:]
    l_out, r_out, u_out, F, C, Ub, Lh, Ll, Lf, T, D, E, Wh, Wl, sem = refs
    rid = ids[8]
    core = ids[9]
    wide = SEP // 2
    copies = []
    for src, half in ((mine, core), (theirs, 1 - core)):
        for r in range(4):
            for side in range(2):
                cols = pl.ds(side * wide, wide)
                sep_at = pl.multiple_of(r * 256 + half * BLK, BLK)
                cpl_at = pl.multiple_of(SEP + r * BLK + half * 64, 64)
                copies.append((src.at[r, pl.ds(side * BLK, BLK), :], F.at[pl.ds(sep_at, BLK), cols]))
                copies.append((src.at[r, pl.ds(256 + side * 64, 64), :], F.at[pl.ds(cpl_at, 64), cols]))
            if level == 0:
                copies.append((src.at[r, pl.ds(384, BLK), :], Ub.at[half, pl.ds(r * BLK, BLK), :]))
    if level > 0:
        copies.append((own_in, Ub.at[0]))
        copies.append((near_in, Ub.at[1, pl.ds(pl.multiple_of(core * 256, 256), 256), :]))
        copies.append((far_in, Ub.at[1, pl.ds(pl.multiple_of((1 - core) * 256, 256), 256), :]))
    copies = [pltpu.make_async_copy(s, t, sem.at[n]) for n, (s, t) in enumerate(copies)]
    for c in copies:
        c.start()
    C[...] = jnp.zeros_like(C)
    Lh[...] = jnp.zeros_like(Lh)
    Ll[...] = jnp.zeros_like(Ll)
    for c in copies:
        c.wait()

    def add_block(t, c):
        child = t // 16
        i = t // 4 % 4
        j = t % 4
        mi = ids[4 * child + i]
        mj = ids[4 * child + j]
        part = Ub[child, blk(i), blk(j)]

        @pl.when(mj < NSEP)
        def _():
            F[blk(mi), blk(mj)] += part

        @pl.when((mj >= NSEP) & (mi >= NSEP))
        def _():
            C[blk(jnp.maximum(mi - NSEP, 0)), blk(jnp.maximum(mj - NSEP, 0))] += part

        return c

    lax.fori_loop(0, 32, add_block, 0)
    D[...] = F[:BLK, :BLK]

    def panel(k, lo):
        th, tl = split(T[lo:, :])
        v = nt3(th, tl, Wh[...], Wl[...])
        Lf[lo:, blk(k)] = v
        h, l = split(v)
        Lh[lo:, blk(k)] = h
        Ll[lo:, blk(k)] = l

    def step(k, lo, depth):
        n = jnp.minimum(k + 1, NSEP - 1)
        panel(jnp.maximum(k - 1, 0), lo)
        T[lo:, :] = F[lo:, blk(k)] - nt3(
            Lh[lo:, :depth], Ll[lo:, :depth], Lh[blk(k), :depth], Ll[blk(k), :depth]
        )
        nh = Lh[blk(n), :depth]
        nl = Ll[blk(n), :depth]
        E[...] = F[blk(n), blk(n)] - nt3(nh, nl, nh, nl)
        W = jnp.concatenate(block_inverse([D[8 * g : 8 * g + 8, :] for g in range(BLK // 8)]), axis=0)
        wh, wl = split(W)
        Wh[...] = wh
        Wl[...] = wl
        th, tl = split(T[blk(n), :])
        h, l = split(nt3(th, tl, wh, wl))
        D[...] = E[...] - nt3(h, l, h, l)

    T[...] = jnp.zeros_like(T)
    Wh[...] = jnp.zeros_like(Wh)
    Wl[...] = jnp.zeros_like(Wl)
    lax.fori_loop(0, 4, lambda k, c: (step(k, 0, 512), c)[1], 0)
    lax.fori_loop(4, 8, lambda k, c: (step(k, 384, 1024), c)[1], 0)
    panel(7, 896)
    rh = Lh[SEP:, :]
    rl = Ll[SEP:, :]
    if level == LEVELS - 1:
        mine = pl.ds(pl.multiple_of(rid * BLK, BLK), BLK)
        mine_l = pl.ds(pl.multiple_of(SEP + rid * BLK, BLK), BLK)
        u_out[...] = C[mine, :] - nt3(Lh[mine_l, :], Ll[mine_l, :], rh, rl)
    else:
        u_out[...] = C[...] - nt3(rh, rl, rh, rl)
    rows = pl.ds(pl.multiple_of(rid * 256, 256), 256)
    ri = lax.broadcasted_iota(jnp.int32, (256, SEP), 0) + rid * 256
    ci = lax.broadcasted_iota(jnp.int32, (256, SEP), 1)
    l_out[...] = jnp.where(ri >= ci, Lf[rows, :], 0.0)
    r_out[...] = Lf[pl.ds(pl.multiple_of(SEP + rid * BLK, BLK), BLK), :]


def front(level, ids, mine, theirs, *updates):
    smem = pl.BlockSpec(memory_space=pltpu.SMEM)
    vmem = pl.BlockSpec(memory_space=pltpu.VMEM)
    hbm = pl.BlockSpec(memory_space=pl.ANY)
    last = level == LEVELS - 1
    copies = 40
    return pl.pallas_call(
        lambda *refs: front_body(level, refs),
        in_specs=[smem] + [hbm] * (2 + len(updates)),
        out_specs=[vmem] * 3,
        out_shape=[
            jax.ShapeDtypeStruct((256, SEP), f32),
            jax.ShapeDtypeStruct((BLK, SEP), f32),
            jax.ShapeDtypeStruct((BLK if last else UPD, UPD), f32),
        ],
        scratch_shapes=[
            pltpu.VMEM((FRONT, SEP), f32),
            pltpu.VMEM((UPD, UPD), f32),
            pltpu.VMEM((2, UPD, UPD), f32),
            pltpu.VMEM((FRONT, SEP), bf16),
            pltpu.VMEM((FRONT, SEP), bf16),
            pltpu.VMEM((FRONT, SEP), f32),
            pltpu.VMEM((FRONT, BLK), f32),
            pltpu.VMEM((BLK, BLK), f32),
            pltpu.VMEM((BLK, BLK), f32),
            pltpu.VMEM((BLK, BLK), bf16),
            pltpu.VMEM((BLK, BLK), bf16),
            pltpu.SemaphoreType.DMA((copies,)),
        ],
        compiler_params=pltpu.CompilerParams(vmem_limit_bytes=48 << 20),
        cost_estimate=pl.CostEstimate(flops=20_000_000_000, transcendentals=0, bytes_accessed=20_000_000),
        name=f"front{level}",
    )(ids, mine, theirs, *updates)


def swap(x, stride):
    return lax.ppermute(x, "leaf", [(i, i ^ 1 << stride) for i in range(lax.axis_size("leaf"))])


def pick(x, half, core):
    return lax.dynamic_slice_in_dim(x, core * half, half, x.ndim - 2)


def pack(sep, cpl, *rest):
    wide = SEP // 2
    return jnp.concatenate([sep[:, :wide], sep[:, wide:], cpl[:, :wide], cpl[:, wide:], *rest], axis=0)


def on_device(child_update, block_maps, sep_share, coupling_share):
    leaf = lax.axis_index("leaf")
    rid = lax.axis_index("rows")
    core = leaf & 1
    sep = sep_share[0]
    cpl = coupling_share[0]

    def pair_sum(levels):
        s = sep[levels]
        c = cpl[levels]
        return (
            pick(s, BLK, core) + swap(pick(s, BLK, 1 - core), 0),
            pick(c, 64, core) + swap(pick(c, 64, 1 - core), 0),
        )

    s0, c0 = pair_sum(slice(0, 1))
    first = lax.all_gather(pack(s0[0], c0[0], child_update[0]), "rows", axis=0, tiled=False)
    s12, c12 = pair_sum(slice(1, 3))
    later = jnp.stack([pack(s12[0], c12[0]), pack(s12[1], c12[1])])
    later = later + swap(later, 1)
    first, later = lax.optimization_barrier((first, later))
    mine = [first, lax.all_gather(later[0], "rows", axis=0, tiled=False), None]
    theirs = [swap(first, 0), None, None]
    p2 = later[1]
    far2 = swap(p2, 2)
    diag_parts = []
    below_parts = []
    current = None
    for level in range(LEVELS):
        own = leaf >> level
        updates = ()
        child_ids = (own, own ^ 1)
        if level == 0:
            child_ids = (own - core, own - core + 1)
        else:
            near = swap(lax.dynamic_slice_in_dim(current, core * 256, 256, 0), level)
            updates = (current, near, swap(near, 0))
            theirs[level] = swap(mine[level], 0)
        ids = jnp.concatenate(
            [lax.dynamic_index_in_dim(block_maps[level], i, 0, keepdims=False) for i in child_ids]
            + [jnp.stack([rid, core]).astype(jnp.int32)]
        )
        l_rows, r_rows, current = front(level, ids, mine[level], theirs[level], *updates)
        if level == 0:
            p2, mine[1], current = lax.optimization_barrier((p2, mine[1], current))
            mine[2] = lax.all_gather(p2 + far2, "rows", axis=0, tiled=False)
        elif level == 1:
            mine[2], current = lax.optimization_barrier((mine[2], current))
        diag_parts.append(l_rows)
        below_parts.append(r_rows)
    return (jnp.stack(diag_parts)[None], jnp.stack(below_parts)[None], current[None])


def solution(mesh):
    return jax.shard_map(
        on_device,
        mesh=mesh,
        in_specs=(
            P("leaf", "rows", None),
            P(),
            P("leaf", None, "rows", None),
            P("leaf", None, "rows", None),
        ),
        out_specs=(
            P("leaf", None, "rows", None),
            P("leaf", None, "rows", None),
            P("leaf", "rows", None),
        ),
        check_vma=False,
    )
```

time: 371 us -> 238 us (0.64); the launches traced: 366 us -> 238 us
  waiting for transfers between devices: 148 us -> 76.9 us
  Pallas kernels: 155 us -> 113 us
  starting transfers between devices: 27.7 us -> 14 us
    all_gather x7 -> x3, waiting for transfers between devices: 89 us -> 8.1 us  [the longest x1 8.07 us: on_device(): lax.all_gather(pack(s0[0], c0[0], child_update[0]), 'rows', axis=0, tiled...]
    pallas_call x3, Pallas kernels: 155 us -> 113 us  [front(): pl.pallas_call(lambda *refs: front_body(level, refs), in_specs=[smem] + [...]
    ppermute x16 -> x13, starting transfers between devices: 27.4 us -> 13.9 us  [swap(): lax.ppermute(x, 'leaf', [(i, i ^ 1 << stride) for i in range(lax.axis_siz...]
    ppermute x16 -> x13, waiting for transfers between devices: 57.9 us -> 68.7 us  [swap(): lax.ppermute(x, 'leaf', [(i, i ^ 1 << stride) for i in range(lax.axis_siz...]
    unnamed x18 -> x20, local copies, waits for them, and re-layouts: 8.44 us -> 5.64 us
  transfers between devices with their start and end apart: 23 -> 16, of which waited for: 17 -> 10; matrix products, arithmetic and copies ran while one was open for 3% -> 4% of each run, Pallas kernels for 28% -> 32%
where the time goes in v2:
time: 238 us
  Pallas kernels  113 us (47%)
  waiting for transfers between devices  76.9 us (32%)
  between operations  14.1 us (6%)
  starting transfers between devices  14 us (6%)
  local copies, waits for them, and re-layouts  12.7 us (5%)
  other arithmetic  6.51 us (3%)
    pallas_call x3, Pallas kernels, front(): pl.pallas_call(lambda *refs: front_body(level, refs), in_specs=[smem] + [...  113 us
    ppermute x13, waiting for transfers between devices, swap(): lax.ppermute(x, 'leaf', [(i, i ^ 1 << stride) for i in range(lax.axis_siz...  68.7 us
    ppermute x13, starting transfers between devices, swap(): lax.ppermute(x, 'leaf', [(i, i ^ 1 << stride) for i in range(lax.axis_siz...  13.9 us
    all_gather x1, waiting for transfers between devices, on_device(): lax.all_gather(pack(s0[0], c0[0], child_update[0]), 'rows', axis=0, tiled...  8.07 us
    unnamed x20, local copies, waits for them, and re-layouts  5.64 us
  transfers between devices with their start and end apart: 16, of which 10 were waited for; matrix products, arithmetic and copies ran while one was open for 4% of the time, Pallas kernels for 32%

profile of v2, /device:TPU:1, one launch (start us, length us, event | category | flops | bytes accessed | tf_op | source)
XLA Modules:
  0.0 237.5 jit_solution(6787640951301223517)
XLA Ops:
  7.2 1.3 slice.83
  8.6 1.5 collective-permute-start
  11.3 1.5 collective-permute-done.1
  14.9 1.4 slice.93
  18.5 1.6 collective-permute-done.2
  20.7 1.5 collective-permute-start.4
  22.2 34.6 %collective-permute-done.4 = f32[2,384,512]{2,1,0:T(8,128)S(1)} collective-permute-done((f32[2,384,512]{2,1,0:T(8,128)S(1)}, f32[2,384,512]{2,1,0:T(8,128)S(1)}, u32[]{:S(2)}, u32[]{:S(2)}) %collective-permute-start.4) | collective-permute-done | bytes 1572896 | tf_op jit(solution)/shard_map/ppermute | solution.py:249
  57.1 8.1 %all-gather.8.cloned.1.call-done = f32[2048,512]{1,0:T(8,128)} async-done(((f32[512,512]{1,0:T(8,128)}), f32[2048,512]{1,0:T(8,128)}) %all-gather.8.cloned.1.call-update) | async-done | bytes 4194320 | tf_op jit(solution)/shard_map/all_gather | solution.py:277
  67.3 2.9 %collective-permute-start.9 = (f32[384,512]{1,0:T(8,128)S(1)}, f32[384,512]{1,0:T(8,128)}, u32[]{:S(2)}, u32[]{:S(2)}) collective-permute-start(f32[384,512]{1,0:T(8,128)S(1)} %get-tuple-element.26), channel_id=1, source_target_pairs={{0,16},{4,20},{8,24},{12,28},{16,0},{20,4},{24,8},{28,12},{32,48},... | collective-permute-start | bytes 2359304 | tf_op jit(solution)/shard_map/ppermute | solution.py:249
  70.2 2.8 %collective-permute-done.5.refs_2_ = f32[4,512,512]{2,1,0:T(8,128)} collective-permute-done((f32[4,512,512]{2,1,0:T(8,128)}, f32[4,512,512]{2,1,0:T(8,128)}, u32[]{:S(2)}, u32[]{:S(2)}) %collective-permute-start.5) | collective-permute-done | bytes 4194336 | tf_op jit(solution)/shard_map/ppermute | solution.py:249
  73.0 38.0 %front0.1 = (f32[256,1024]{1,0:T(8,128)S(1)}, f32[128,1024]{1,0:T(8,128)S(1)}, f32[512,512]{1,0:T(8,128)S(1)}) custom-call(s32[10]{0:T(128)S(1)} %add_add_fusion.refs_0_, f32[4,512,512]{2,1,0:T(8,128)} %bitcast.62, f32[4,512,512]{2,1,0:T(8,128)} %collective-permute-done.5.refs_2_), custom_call_target="tpu_custom_call" | custom-call | flops 20000000000 | bytes 20000000 | tf_op jit(solution)/shard_map/front0/pallas_call | solution.py:219
  111.5 2.2 add.79
  113.7 1.3 collective-permute-start.7
  115.0 12.1 %collective-permute-done.7.refs_4_ = f32[256,512]{1,0:T(8,128)S(1)} collective-permute-done((f32[256,512]{1,0:T(8,128)S(1)}, f32[256,512]{1,0:T(8,128)S(1)}, u32[]{:S(2)}, u32[]{:S(2)}) %collective-permute-start.7) | collective-permute-done | bytes 524320 | tf_op jit(solution)/shard_map/ppermute | solution.py:249
  128.2 1.5 collective-permute-done.8.refs_5_
  129.7 1.2 copy-done.3
  130.9 37.4 %front1.1 = (f32[256,1024]{1,0:T(8,128)S(1)}, f32[128,1024]{1,0:T(8,128)S(1)}, f32[512,512]{1,0:T(8,128)S(1)}) custom-call(s32[10]{0:T(128)S(1)} %add_add_fusion.1.refs_0_, f32[4,384,512]{2,1,0:T(8,128)} %all-gather.6.cloned.1.call-done.refs_1_, f32[4,384,512]{2,1,0:T(8,128)} %collective-permute-done.6.refs_2_, f32[512,512]{1,0:T(8,128)S(1)} %copy-done.3, ...), custom_call_target="tpu_custom_call" | custom-call | flops 20000000000 | bytes 20000000 | tf_op jit(solution)/shard_map/front1/pallas_call | solution.py:219
  170.8 2.7 %collective-permute-start.11 = (f32[256,512]{1,0:T(8,128)S(1)}, f32[256,512]{1,0:T(8,128)}, u32[]{:S(2)}, u32[]{:S(2)}) collective-permute-start(f32[256,512]{1,0:T(8,128)S(1)} %constant_dynamic-slice_fusion), channel_id=1, source_target_pairs={{0,16},{4,20},{8,24},{12,28},{16,0},{20,4},{24,8},{28,12},{32,48},... | collective-permute-start | bytes 1572872 | tf_op jit(solution)/shard_map/ppermute | solution.py:249
  173.5 12.3 %collective-permute-done.11.refs_4_ = f32[256,512]{1,0:T(8,128)} collective-permute-done((f32[256,512]{1,0:T(8,128)S(1)}, f32[256,512]{1,0:T(8,128)}, u32[]{:S(2)}, u32[]{:S(2)}) %collective-permute-start.11) | collective-permute-done | bytes 524320 | tf_op jit(solution)/shard_map/ppermute | solution.py:249
  187.1 1.6 collective-permute-done.12.refs_5_
  188.7 1.2 copy-done.1
  189.9 37.9 %front2.1 = (f32[256,1024]{1,0:T(8,128)S(1)}, f32[128,1024]{1,0:T(8,128)S(1)}, f32[128,512]{1,0:T(8,128)}) custom-call(s32[10]{0:T(128)S(1)} %add_add_fusion.2.refs_0_, f32[4,384,512]{2,1,0:T(8,128)} %bitcast.64, f32[4,384,512]{2,1,0:T(8,128)} %collective-permute-done.10.refs_2_, f32[512,512]{1,0:T(8,128)S(1)} %copy-done.1, ...), custom_call_target="tpu_custom_call" | custom-call | flops 20000000000 | bytes 20000000 | tf_op jit(solution)/shard_map/front2/pallas_call | solution.py:219
  227.8 1.3 maximum_bitcast_fusion.1
  229.0 1.9 maximum_bitcast_fusion
  (67 shorter events, 13.7 us)
Async XLA Ops:
  7.2 58.0 %all-gather.8.cloned.1.call-start = ((), (), s32[]{:S(2)}) async-start(), calls=%async_computation.1 | async-start | bytes 5242880 | tf_op jit(solution)/shard_map/all_gather | solution.py:277
  8.6 4.3 %collective-permute-start = (f32[1,128,1024]{2,1,0:T(8,128)S(1)}, f32[1,128,1024]{2,1,0:T(8,128)S(1)}, u32[]{:S(2)}, u32[]{:S(2)}) collective-permute-start(f32[1,128,1024]{2,1,0:T(8,128)S(1)} %dynamic-slice_bitcast_fusion.2), channel_id=1, source_target_pairs={{0,4},{4,0},{8,12},{12,8},{16,20},{20,16},{24,28},{28,24},{32,36},... | collective-permute-start | bytes 1572872 | tf_op jit(solution)/shard_map/ppermute | solution.py:249
  11.2 1.6 collective-permute-start.1
  12.8 1.0 copy-start.6
  13.8 1.0 copy-start.5
  14.8 2.2 copy-start.4
  14.8 96.2 %all-gather.6.cloned.1.call-start = ((), (), s32[]{:S(2)}) async-start(), calls=%async_computation | async-start | bytes 3932160 | tf_op jit(solution)/shard_map/all_gather | solution.py:282
  16.4 2.0 collective-permute-start.3
  17.4 2.7 %collective-permute-start.2 = (f32[2,128,1024]{2,1,0:T(8,128)S(1)}, f32[2,128,1024]{2,1,0:T(8,128)S(1)}, u32[]{:S(2)}, u32[]{:S(2)}) collective-permute-start(f32[2,128,1024]{2,1,0:T(8,128)S(1)} %dynamic-slice_bitcast_fusion), channel_id=1, source_target_pairs={{0,4},{4,0},{8,12},{12,8},{16,20},{20,16},{24,28},{28,24},{32,36},... | collective-permute-start | bytes 3145736 | tf_op jit(solution)/shard_map/ppermute | solution.py:249
  20.7 36.0 %collective-permute-start.4 = (f32[2,384,512]{2,1,0:T(8,128)S(1)}, f32[2,384,512]{2,1,0:T(8,128)S(1)}, u32[]{:S(2)}, u32[]{:S(2)}) collective-permute-start(f32[2,384,512]{2,1,0:T(8,128)S(1)} %pad_maximum_fusion), channel_id=1, source_target_pairs={{0,8},{4,12},{8,0},{12,4},{16,24},{20,28},{24,16},{28,20},{32,40},... | collective-permute-start | bytes 4718600 | tf_op jit(solution)/shard_map/ppermute | solution.py:249
  65.2 1.8 copy-start.7
  65.2 7.8 %collective-permute-start.5 = (f32[4,512,512]{2,1,0:T(8,128)}, f32[4,512,512]{2,1,0:T(8,128)}, u32[]{:S(2)}, u32[]{:S(2)}) collective-permute-start(f32[4,512,512]{2,1,0:T(8,128)} %bitcast.61), channel_id=1, source_target_pairs={{0,4},{4,0},{8,12},{12,8},{16,20},{20,16},{24,28},{28,24},{32,36},... | collective-permute-start | bytes 12582920 | tf_op jit(solution)/shard_map/ppermute | solution.py:249
  66.9 102.5 %all-gather.10.cloned.1.call-start = ((), (), s32[]{:S(2)}) async-start(), calls=%async_computation.2 | async-start | bytes 3932160 | tf_op jit(solution)/shard_map/all_gather | solution.py:306
  67.3 44.2 %collective-permute-start.9 = (f32[384,512]{1,0:T(8,128)S(1)}, f32[384,512]{1,0:T(8,128)}, u32[]{:S(2)}, u32[]{:S(2)}) collective-permute-start(f32[384,512]{1,0:T(8,128)S(1)} %get-tuple-element.26), channel_id=1, source_target_pairs={{0,16},{4,20},{8,24},{12,28},{16,0},{20,4},{24,8},{28,12},{32,48},... | collective-permute-start | bytes 2359304 | tf_op jit(solution)/shard_map/ppermute | solution.py:249
  111.0 2.7 %copy-start.2 = (f32[512,512]{1,0:T(8,128)}, f32[512,512]{1,0:T(8,128)S(1)}, u32[]{:S(2)}) copy-start(f32[512,512]{1,0:T(8,128)S(1)} %get-tuple-element.24.refs_3_) | copy-start | bytes 3145732
  111.0 18.6 %collective-permute-start.6 = (f32[4,384,512]{2,1,0:T(8,128)}, f32[4,384,512]{2,1,0:T(8,128)}, u32[]{:S(2)}, u32[]{:S(2)}) collective-permute-start(f32[4,384,512]{2,1,0:T(8,128)} %all-gather.6.cloned.1.call-done.refs_1_), channel_id=1, source_target_pairs={{0,4},{4,0},{8,12},{12,8},{16,20},{20,16},{24,28},{28,24},{32,36},... | collective-permute-start | bytes 9437192 | tf_op jit(solution)/shard_map/ppermute | solution.py:249
  113.7 13.3 %collective-permute-start.7 = (f32[256,512]{1,0:T(8,128)S(1)}, f32[256,512]{1,0:T(8,128)S(1)}, u32[]{:S(2)}, u32[]{:S(2)}) collective-permute-start(f32[256,512]{1,0:T(8,128)S(1)} %constant_dynamic-slice_fusion.3), channel_id=1, source_target_pairs={{0,8},{4,12},{8,0},{12,4},{16,24},{20,28},{24,16},{28,20},{32,40},... | collective-permute-start | bytes 1572872 | tf_op jit(solution)/shard_map/ppermute | solution.py:249
  127.1 2.6 %collective-permute-start.8 = (f32[256,512]{1,0:T(8,128)S(1)}, f32[256,512]{1,0:T(8,128)S(1)}, u32[]{:S(2)}, u32[]{:S(2)}) collective-permute-start(f32[256,512]{1,0:T(8,128)S(1)} %collective-permute-done.7.refs_4_), channel_id=1, source_target_pairs={{0,4},{4,0},{8,12},{12,8},{16,20},{20,16},{24,28},{28,24},{32,36},... | collective-permute-start | bytes 1572872 | tf_op jit(solution)/shard_map/ppermute | solution.py:249
  129.7 1.2 copy-start.3
  168.3 1.0 copy-start
  169.3 19.4 %collective-permute-start.10 = (f32[4,384,512]{2,1,0:T(8,128)}, f32[4,384,512]{2,1,0:T(8,128)}, u32[]{:S(2)}, u32[]{:S(2)}) collective-permute-start(f32[4,384,512]{2,1,0:T(8,128)} %bitcast.63), channel_id=1, source_target_pairs={{0,4},{4,0},{8,12},{12,8},{16,20},{20,16},{24,28},{28,24},{32,36},... | collective-permute-start | bytes 9437192 | tf_op jit(solution)/shard_map/ppermute | solution.py:249
  170.8 15.1 %collective-permute-start.11 = (f32[256,512]{1,0:T(8,128)S(1)}, f32[256,512]{1,0:T(8,128)}, u32[]{:S(2)}, u32[]{:S(2)}) collective-permute-start(f32[256,512]{1,0:T(8,128)S(1)} %constant_dynamic-slice_fusion), channel_id=1, source_target_pairs={{0,16},{4,20},{8,24},{12,28},{16,0},{20,4},{24,8},{28,12},{32,48},... | collective-permute-start | bytes 1572872 | tf_op jit(solution)/shard_map/ppermute | solution.py:249
  185.8 2.8 %collective-permute-start.12 = (f32[256,512]{1,0:T(8,128)}, f32[256,512]{1,0:T(8,128)}, u32[]{:S(2)}, u32[]{:S(2)}) collective-permute-start(f32[256,512]{1,0:T(8,128)} %collective-permute-done.11.refs_4_), channel_id=1, source_target_pairs={{0,4},{4,0},{8,12},{12,8},{16,20},{20,16},{24,28},{28,24},{32,36},... | collective-permute-start | bytes 1572872 | tf_op jit(solution)/shard_map/ppermute | solution.py:249
  188.7 1.2 copy-start.1
Sparse Core Ops, SparseCore 0:
  14.9 50.1 all-gather.7
  67.4 39.8 all-gather.5
  113.8 39.3 all-gather.9
